TPU v7x, 128 devices: a whole 4x4x4 slice. The times are simulated.
128 devices in a mesh: dp: 64 (over z, y_hi, x, core), mp: 2 (over y_lo).
Axes of the slice: x: 4, y: 4 (y_hi: 2, y_lo: 2; y = y_hi * 2 + y_lo), z: 4, core: 2. Of those that a mesh axis runs over, the one named last changes fastest.
Arguments:
- tokens: bfloat16 [25600, 1792], P('dp', 'mp'), may hold values from -6 to 6
- cotangent: bfloat16 [25600, 1792], P('dp', 'mp'), may hold values from -6 to 6
- master: float32 [1792, 4, 1792], P('dp', None, 'mp')
- moment_one: float32 [1792, 4, 1792], P('dp', None, 'mp'), may hold values from -4 to 4
- moment_two: float32 [1792, 4, 1792], P('dp', None, 'mp'), may hold values from 0.01 to 1
- ln_gain: float32 [1792], replicated, may hold values from 0.1 to 1.9
- ln_bias: float32 [1792], replicated, may hold values from -3 to 3
- norm_moment_one: float32 [2, 1792], replicated, may hold values from -4 to 4
- norm_moment_two: float32 [2, 1792], replicated, may hold values from 0.01 to 1
- image_count: int32 [64], P('dp'), may hold values from 1 to 25, as said below
- tokens_per_image: int32 [64], P('dp'), may hold values from 16 to 400, as said below
Outputs:
- block_out: bfloat16 [25600, 1792], P('dp', 'mp')
- input_grad: bfloat16 [25600, 1792], P('dp', 'mp')
- new_master: float32 [1792, 4, 1792], P('dp', None, 'mp')
- new_moment_one: float32 [1792, 4, 1792], P('dp', None, 'mp')
- new_moment_two: float32 [1792, 4, 1792], P('dp', None, 'mp')
- new_gain: float32 [1792], replicated
- new_bias: float32 [1792], replicated
- new_norm_moment_one: float32 [2, 1792], replicated
- new_norm_moment_two: float32 [2, 1792], replicated
Inputs may be any that keep to these rules, and one draw needn't show every extreme that they name: `tokens_per_image`: A square number s * s; some group has exactly 400. image_count[g] * tokens_per_image[g] is at most 400 for every group g.
All inputs are finite; a program needn't handle non-finite values.
Results may differ from a plain program's by a relative error of at most 0.0085.
Values may be sent and summed in bfloat16 or wider, within the bound.
A program may use at most 192 MiB of HBM per device.

v0:
```python
import jax
import jax.numpy as jnp
from jax import lax
from jax.sharding import Mesh
from jax.sharding import PartitionSpec as P

HEAD_DIM = 112
DP = ("dp_0", "dp_1", "dp_2", "dp_3")
DP_MP = ("dp_0", "dp_1", "dp_2", "dp_3", "mp")


eps_norm = 1e-06
beta_one = 0.9
beta_two = 0.95
learn_rate = 0.01
decay_rate = 0.1
adam_eps = 1e-08
step_count = 10.0


def split_up(shard, dim, length):
    dims = shard.shape
    parts = shard.reshape(*dims[:dim], length, dims[dim] // length, *dims[dim + 1 :])
    return jnp.moveaxis(parts, dim, 0)


def summed_on_arrival(shard, axis, dim):
    length = lax.axis_size(axis)
    parts = lax.all_to_all(split_up(shard, dim, length), axis, 0, 0, tiled=True)
    return jnp.sum(parts.astype(jnp.float32), axis=0)


def sum_by_chip(shard, chips, core, dim):
    sizes = (lax.axis_size(chips), lax.axis_size(core))
    parts = split_up(shard, dim, sizes[0] * sizes[1])
    inside = parts.shape[1:]
    parts = parts.reshape(*sizes, *inside).swapaxes(0, 1).reshape(-1, *inside)
    parts = lax.psum_scatter(parts, core, scatter_dimension=0, tiled=True)
    return lax.psum_scatter(parts, chips, scatter_dimension=0, tiled=True)[0]


def layer_norm(row_block, gain, shift):
    values = row_block.astype(jnp.float32)
    center = jnp.mean(values, axis=-1, keepdims=True)
    shifted = values - center
    spread = jnp.mean(shifted * shifted, axis=-1, keepdims=True)
    inverse = lax.rsqrt(spread + eps_norm)
    normed = shifted * inverse
    return (normed, inverse, (normed * gain + shift).astype(jnp.bfloat16))


def same_image(image_here, length_here, total_rows):
    places = jnp.arange(total_rows, dtype=jnp.int32)
    live_rows = places < image_here * length_here
    labels = jnp.where(live_rows, places // length_here, jnp.int32(-1))
    return (live_rows, labels[:, None] == labels[None, :])


def adam_update(weight_now, moment_first, moment_second, gradient, decay):
    first_new = beta_one * moment_first + (1.0 - beta_one) * gradient
    second_new = beta_two * moment_second + (1.0 - beta_two) * gradient * gradient
    first_hat = first_new / (1.0 - beta_one**step_count)
    second_hat = second_new / (1.0 - beta_two**step_count)
    weight_new = weight_now - learn_rate * (
        first_hat / (jnp.sqrt(second_hat) + adam_eps) + decay * weight_now
    )
    return (weight_new, first_new, second_new)


def shards(
    tokens,
    cotangent,
    master,
    moment_one,
    moment_two,
    ln_gain,
    ln_bias,
    norm_moment_one,
    norm_moment_two,
    image_count,
    tokens_per_image,
):
    groups = lax.axis_size(DP)
    full_tokens, full_cot = (
        lax.all_gather(tokens, "mp", axis=1, tiled=True),
        lax.all_gather(cotangent, "mp", axis=1, tiled=True),
    )
    row_count = full_tokens.shape[0]
    normed, inverse, normed_low = layer_norm(full_tokens, ln_gain, ln_bias)
    live_rows, allowed = same_image(image_count[0], tokens_per_image[0], row_count)
    weights = lax.all_gather(master.astype(jnp.bfloat16), DP, axis=0, tiled=True)
    heads_here = weights.shape[2] // HEAD_DIM
    score_scale = HEAD_DIM ** (-0.5)
    projected = jnp.einsum(
        "td,dkh->kth", normed_low, weights[:, :3], preferred_element_type=jnp.float32
    ).astype(jnp.bfloat16)
    query_rows = projected[0].reshape(row_count, heads_here, HEAD_DIM)
    key_rows = projected[1].reshape(row_count, heads_here, HEAD_DIM)
    value_rows = projected[2].reshape(row_count, heads_here, HEAD_DIM)
    scores = (
        jnp.einsum("qhd,khd->hqk", query_rows, key_rows, preferred_element_type=jnp.float32)
        * score_scale
    )
    scores = jnp.where(allowed[None], scores, -1e30)
    row_max = jnp.max(scores, axis=-1, keepdims=True)
    raised = jnp.exp(scores - row_max)
    prob_full = raised / jnp.sum(raised, axis=-1, keepdims=True)
    prob_half = prob_full.astype(jnp.bfloat16)
    mixed = jnp.einsum(
        "hqk,khd->qhd", prob_half, value_rows, preferred_element_type=jnp.float32
    ).astype(jnp.bfloat16)
    mixed = mixed.reshape(row_count, heads_here * HEAD_DIM)
    out_weight = weights[:, 3]
    out_part = lax.dot_general(
        mixed, out_weight, (((1,), (1,)), ((), ())), preferred_element_type=jnp.float32
    )
    out_sum = lax.psum_scatter(
        out_part.astype(jnp.bfloat16), "mp", scatter_dimension=1, tiled=True
    ).astype(jnp.float32)
    block_out = (tokens.astype(jnp.float32) + out_sum).astype(jnp.bfloat16)
    live_column = live_rows[:, None]
    grad_full = jnp.where(live_column, full_cot, jnp.zeros_like(full_cot))
    mixed_grad = jnp.dot(grad_full, out_weight, preferred_element_type=jnp.float32).astype(
        jnp.bfloat16
    )
    mixed_grad = mixed_grad.reshape(row_count, heads_here, HEAD_DIM)
    prob_grad = jnp.einsum(
        "qhd,khd->hqk", mixed_grad, value_rows, preferred_element_type=jnp.float32
    )
    value_grad = jnp.einsum(
        "hqk,qhd->khd", prob_half, mixed_grad, preferred_element_type=jnp.float32
    ).astype(jnp.bfloat16)
    delta = jnp.sum(prob_full * prob_grad, axis=-1, keepdims=True)
    score_grad = (prob_full * (prob_grad - delta) * score_scale).astype(jnp.bfloat16)
    query_grad = jnp.einsum(
        "hqk,khd->qhd", score_grad, key_rows, preferred_element_type=jnp.float32
    ).astype(jnp.bfloat16)
    key_grad = jnp.einsum(
        "hqk,qhd->khd", score_grad, query_rows, preferred_element_type=jnp.float32
    ).astype(jnp.bfloat16)
    proj_grad = jnp.stack([query_grad, key_grad, value_grad]).reshape(
        3, row_count, heads_here * HEAD_DIM
    )
    norm_grad = jnp.einsum(
        "kth,dkh->td", proj_grad, weights[:, :3], preferred_element_type=jnp.float32
    )
    gain_part = jnp.sum(norm_grad * normed, axis=0)
    bias_part = jnp.sum(norm_grad, axis=0)
    scaled = norm_grad * ln_gain
    input_part = inverse * (
        scaled
        - jnp.mean(scaled, axis=-1, keepdims=True)
        - normed * jnp.mean(scaled * normed, axis=-1, keepdims=True)
    )
    input_sum = summed_on_arrival(input_part.astype(jnp.bfloat16), "mp", 1)
    grad_local = jnp.where(live_column, cotangent, jnp.zeros_like(cotangent))
    input_grad = (grad_local.astype(jnp.float32) + input_sum).astype(jnp.bfloat16)
    gain_sum, bias_sum = lax.psum((gain_part, bias_part), DP_MP)
    inner_piece = jnp.einsum(
        "td,kth->dkh", normed_low, proj_grad, preferred_element_type=jnp.float32
    )
    outer_piece = lax.dot_general(
        grad_full, mixed, (((0,), (0,)), ((), ())), preferred_element_type=jnp.float32
    )
    grad_shard = sum_by_chip(
        jnp.concatenate([inner_piece, outer_piece[:, None]], axis=1),
        ("dp_0", "dp_1", "dp_2"),
        "dp_3",
        0,
    )
    weight_grad = grad_shard / groups
    new_master, new_moment_one, new_moment_two = adam_update(
        master, moment_one, moment_two, weight_grad, decay_rate
    )
    norm_param_grad = jnp.stack([gain_sum, bias_sum]) / groups
    stacked_params = jnp.stack([ln_gain, ln_bias])
    new_norm, new_norm_moment_one, new_norm_moment_two = adam_update(
        stacked_params, norm_moment_one, norm_moment_two, norm_param_grad, 0.0
    )
    return (
        block_out,
        input_grad,
        new_master,
        new_moment_one,
        new_moment_two,
        new_norm[0],
        new_norm[1],
        new_norm_moment_one,
        new_norm_moment_two,
    )


def solution(mesh):
    finer = Mesh(
        mesh.devices.reshape(4, 2, 4, 2, mesh.shape["mp"]), ("dp_0", "dp_1", "dp_2", "dp_3", "mp")
    )
    return jax.shard_map(
        shards,
        mesh=finer,
        in_specs=(
            P(DP, "mp"),
            P(DP, "mp"),
            P(DP, None, "mp"),
            P(DP, None, "mp"),
            P(DP, None, "mp"),
            P(),
            P(),
            P(),
            P(),
            P(DP),
            P(DP),
        ),
        out_specs=(
            P(DP, "mp"),
            P(DP, "mp"),
            P(DP, None, "mp"),
            P(DP, None, "mp"),
            P(DP, None, "mp"),
            P(),
            P(),
            P(),
            P(),
        ),
        check_vma=False,
    )
```

profile of v0, /device:TPU:0, one launch (start us, length us, event | category | flops | bytes accessed | tf_op | source)
XLA Modules:
  0.0 827.0 jit_solution(15908292925435911702)
XLA Ops:
  12.2 28.1 %all-gather.8.cloned.1.call-done = bf16[400,1792]{1,0:T(8,128)(2,1)} async-done(((bf16[400,896]{1,0:T(8,128)(2,1)}), bf16[400,1792]{1,0:T(8,128)(2,1)}) %all-gather.8.cloned.1.call-update) | async-done | bytes 1433616 | tf_op jit(solution)/shard_map/all_gather | solution.py:86
  44.7 26.4 %all-gather.4.cloned.1.call-done = bf16[400,1792]{1,0:T(8,128)(2,1)} async-done(((bf16[400,896]{1,0:T(8,128)(2,1)}), bf16[400,1792]{1,0:T(8,128)(2,1)}) %all-gather.4.cloned.1.call-update) | async-done | bytes 1433616 | tf_op jit(solution)/shard_map/all_gather | solution.py:85
  74.7 95.3 %all-gather.6.cloned.1.call-done = bf16[1792,4,896]{2,1,0:T(4,128)(2,1)} async-done(((bf16[28,4,896]{2,1,0:T(4,128)(2,1)}), bf16[1792,4,896]{2,1,0:T(4,128)(2,1)}) %all-gather.6.cloned.1.call-update) | async-done | bytes 12845072 | tf_op jit(solution)/shard_map/all_gather | solution.py:91
  170.1 9.2 %convert_bitcast_fusion = bf16[3,400,896]{2,1,0:T(8,128)(2,1)S(1)} fusion(bf16[1792,3,896]{2,1,0:T(4,128)(2,1)} %bitcast.61, bf16[400,1792]{1,0:T(8,128)(2,1)S(1)} %copy-done, f32[1792]{0:T(1024)S(1)} %copy-done.20, f32[1792]{0:T(1024)S(1)} %copy-done.17, f32[400]{0:T(512)S(1)} %add_rsqrt_fusion, f32[400]{0:T(512)S(1)} %broadcast_multiply_fusion.2), kind=kOutput, calls=%fused_computation.41 | convolution fusion | flops 3858892800 | bytes 13235328 | tf_op jit(solution)/shard_map/td,dkh->kth/dot_general | solution.py:94
  186.4 8.9 %slice.33 = bf16[1792,1,896]{2,1,0:T(2,128)(2,1)S(1)} slice(bf16[1792,4,896]{2,1,0:T(4,128)(2,1)} %all-gather.6.cloned.1.call-done), slice={[0:1792], [3:4], [0:896]} | slice | bytes 6422528 | tf_op jit(solution)/shard_map/slice | solution.py:113
  205.4 3.1 fusion.93
  208.5 4.2 fusion.69
  215.5 12.7 %fusion.65 = bf16[400,8,112]{2,0,1:T(8,128)(2,1)} fusion(f32[8,400,400]{1,2,0:T(8,128)} %fusion.69, bf16[400,8,112]{2,1,0:T(8,128)(2,1)S(1)} %reshape_squeeze.11, f32[8,400,400]{1,2,0:T(8,128)} %copy-done.22, f32[8,400]{1,0:T(8,128)S(1)} %get-tuple-element.26), kind=kOutput, calls=%fused_computation.60 | convolution fusion | flops 296041984 | bytes 11686400 | tf_op jit(solution)/shard_map/hqk,khd->qhd/dot_general | solution.py:135
  228.2 11.0 %fusion.62 = bf16[400,8,112]{2,0,1:T(8,128)(2,1)} fusion(f32[8,400,400]{1,2,0:T(8,128)} %fusion.69, bf16[400,8,112]{2,1,0:T(8,128)(2,1)S(1)} %copy-done.2, f32[8,400,400]{1,2,0:T(8,128)} %copy-done.22, f32[8,400]{1,0:T(8,128)S(1)} %get-tuple-element.26), kind=kOutput, calls=%fused_computation.59 | convolution fusion | flops 296041984 | bytes 11686400 | tf_op jit(solution)/shard_map/hqk,qhd->khd/dot_general | solution.py:138
  239.2 4.9 fusion.56
  254.5 4.2 convolution_bitcast_fusion
  258.8 6.7 copy.112
  267.1 9.8 %fusion.80 = f32[1792,3,896]{2,0,1:T(8,128)} fusion(bf16[3,400,896]{2,1,0:T(8,128)(2,1)S(1)} %constant_dynamic-update-slice_fusion, bf16[400,1792]{1,0:T(8,128)(2,1)S(1)} %copy-done, f32[1792]{0:T(1024)S(1)} %copy-done.20, f32[1792]{0:T(1024)S(1)} %copy-done.17, f32[400]{0:T(512)S(1)} %add_rsqrt_fusion, f32[400]{0:T(512)S(1)} %broadcast_multiply_fusion.2), kind=kOutput, calls=%fused_computation.74 | convolution fusion | flops 3857817600 | bytes 22869120 | tf_op jit(solution)/shard_map/td,kth->dkh/dot_general | solution.py:159
  276.9 21.7 %concatenate.7 = f32[32,2,28,3,896]{4,2,1,0,3:T(8,128)} reshape(f32[1792,3,896]{2,0,1:T(8,128)} %fusion.80) | data formatting | bytes 38535168 | tf_op jit(solution)/shard_map/concatenate | solution.py:166
  298.6 11.8 %maximum_bitcast_fusion = f32[2,32,28,4,896]{4,2,0,1,3:T(8,128)S(1)} fusion(f32[32,2,28,1,896]{4,2,1,0,3:T(8,128)} %copy.112, f32[32,2,28,3,896]{4,2,1,0,3:T(8,128)} %concatenate.7), kind=kLoop, calls=%fused_computation.2 | loop fusion | flops 6422528 | bytes 51380224 | tf_op jit(solution)/shard_map/transpose | solution.py:37
  310.4 27.8 %copy.113 = f32[2,32,28,4,896]{4,1,0,3,2:T(8,128)} copy(f32[2,32,28,4,896]{4,2,0,1,3:T(8,128)S(1)} %maximum_bitcast_fusion) | data formatting | bytes 51380224 | tf_op jit(solution)/shard_map/transpose | solution.py:37
  339.8 4.7 convolution_convert_fusion
  347.0 22.6 %reduce-scatter.5.cloned.1.call-done = f32[32,28,4,896]{3,0,2,1:T(8,128)} async-done(((f32[64,28,4,896]{3,0,2,1:T(8,128)}), f32[32,28,4,896]{3,0,2,1:T(8,128)}) %reduce-scatter.5.cloned.1.call-update) | async-done | bytes 12845072 | tf_op jit(solution)/shard_map/reduce_scatter | solution.py:38
  369.6 17.2 %copy.114 = f32[32,28,4,896]{3,2,1,0:T(4,128)} copy(f32[32,28,4,896]{3,0,2,1:T(8,128)} %reduce-scatter.5.cloned.1.call-done) | data formatting | bytes 25690112 | tf_op jit(solution)/shard_map/reduce_scatter | solution.py:38
  386.8 10.4 %fusion.34 = (f32[1792]{0:T(1024)S(1)}, f32[400]{0:T(512)S(1)}, f32[400]{0:T(512)S(1)}, f32[1792]{0:T(1024)S(1)}, f32[400,1792]{1,0:T(8,128)S(1)}) fusion(bf16[400,1792]{1,0:T(8,128)(2,1)S(1)} %copy-done, f32[400]{0:T(512)S(1)} %add_rsqrt_fusion, f32[400]{0:T(512)S(1)} %broadcast_multiply_fusion.2, f32[1792]{0:T(1024)S(1)} %copy-done.17, ...), kind=kOutput, calls=%fused_computation.35 | convolution fusion | flops 3860680192 | bytes 16112896 | tf_op jit(solution)/shard_map/kth,dkh->td/dot_general | solution.py:144
  399.5 3.8 all-to-all-start
  404.0 110.0 %all-reduce.1 = (f32[1,1792]{1,0:T(1,128)S(1)}, f32[1,1792]{1,0:T(1,128)S(1)}) all-reduce(f32[1,1792]{1,0:T(1,128)S(1)} %stack.32, f32[1,1792]{1,0:T(1,128)S(1)} %stack.31), channel_id=1, replica_groups=mesh['dp_0'=4,'dp_1'=2,'dp_2'=4,'dp_3'=2,'mp'=2] {'dp_0','dp_1','dp_2','..., use_global_device_ids=true, to_apply=%region_14.15 | all-reduce | flops 3584 | bytes 28672 | tf_op jit(solution)/shard_map/psum | solution.py:158
  519.6 296.8 %all-reduce.4.cloned.1.call-done = f32[32,28,4,896]{3,2,1,0:T(4,128)} async-done(((f32[32,28,4,896]{3,2,1,0:T(4,128)}), f32[32,28,4,896]{3,2,1,0:T(4,128)}) %all-reduce.4.cloned.1.call-update) | async-done | bytes 12845072
  816.4 3.3 multiply_subtract_fusion
  (106 shorter events, 56.2 us)
Async XLA Ops:
  7.2 33.1 %all-gather.8.cloned.1.call-start = ((), (), s32[]{:S(2)}) async-start(), calls=%async_computation.5 | async-start | bytes 2150400 | tf_op jit(solution)/shard_map/all_gather | solution.py:86
  7.9 63.2 %all-gather.4.cloned.1.call-start = ((), (), s32[]{:S(2)}) async-start(), calls=%async_computation.3 | async-start | bytes 2150400 | tf_op jit(solution)/shard_map/all_gather | solution.py:85
  8.7 161.4 %all-gather.6.cloned.1.call-start = ((), (), s32[]{:S(2)}) async-start(), calls=%async_computation.4 | async-start | bytes 13045760 | tf_op jit(solution)/shard_map/all_gather | solution.py:91
  10.5 359.1 %reduce-scatter.5.cloned.1.call-start = ((), (), s32[]{:S(2)}) async-start(), calls=%async_computation.6 | async-start | bytes 38535168 | tf_op jit(solution)/shard_map/reduce_scatter | solution.py:38
  43.1 126.9 %copy-start.17 = (f32[1792]{0:T(1024)S(1)}, f32[1792]{0:T(1024)}, u32[]{:S(2)}) copy-start(f32[1792]{0:T(1024)} %param.16) | copy-start | bytes 21508
  43.1 126.9 %copy-start.20 = (f32[1792]{0:T(1024)S(1)}, f32[1792]{0:T(1024)}, u32[]{:S(2)}) copy-start(f32[1792]{0:T(1024)} %param.17) | copy-start | bytes 21508
  71.1 99.0 %copy-start = (bf16[400,1792]{1,0:T(8,128)(2,1)S(1)}, bf16[400,1792]{1,0:T(8,128)(2,1)}, u32[]{:S(2)}) copy-start(bf16[400,1792]{1,0:T(8,128)(2,1)} %all-gather.4.cloned.1.call-done) | copy-start | bytes 4300804
  186.4 11.5 %copy-start.10 = (bf16[400,1792]{1,0:T(8,128)(2,1)S(1)}, bf16[400,1792]{1,0:T(8,128)(2,1)}, u32[]{:S(2)}) copy-start(bf16[400,1792]{1,0:T(8,128)(2,1)} %all-gather.8.cloned.1.call-done) | copy-start | bytes 4300804
  215.5 12.7 %copy-start.2 = (bf16[400,8,112]{2,1,0:T(8,128)(2,1)S(1)}, bf16[400,8,112]{2,1,0:T(8,128)(2,1)}, u32[]{:S(2)}) copy-start(bf16[400,8,112]{2,1,0:T(8,128)(2,1)} %reshape_squeeze.10) | copy-start | bytes 2150404
  228.2 11.0 %copy-start.4 = (bf16[400,8,112]{2,1,0:T(8,128)(2,1)S(1)}, bf16[400,8,112]{2,1,0:T(8,128)(2,1)}, u32[]{:S(2)}) copy-start(bf16[400,8,112]{2,1,0:T(8,128)(2,1)} %reshape.139) | copy-start | bytes 2150404
  239.2 5.1 copy-start.12
  258.8 6.7 copy-start.6
  258.8 6.7 copy-start.15
  258.8 6.8 copy-start.7
  338.2 178.5 %reduce-scatter.7.cloned.1.call-start = ((), (), s32[]{:S(2)}) async-start(), calls=%async_computation.7 | async-start | bytes 2752512
  347.0 469.4 %all-reduce.4.cloned.1.call-start = ((), (), s32[]{:S(2)}) async-start(), calls=%async_computation.8 | async-start | bytes 25690112
  398.2 5.1 copy-start.21
  398.2 115.8 %copy-start.18 = (f32[2,1792]{1,0:T(2,128)S(1)}, f32[2,1792]{1,0:T(2,128)}, u32[]{:S(2)}) copy-start(f32[2,1792]{1,0:T(2,128)} %param.18) | copy-start | bytes 43012
  398.2 115.8 %copy-start.19 = (f32[2,1792]{1,0:T(2,128)S(1)}, f32[2,1792]{1,0:T(2,128)}, u32[]{:S(2)}) copy-start(f32[2,1792]{1,0:T(2,128)} %param.19) | copy-start | bytes 43012
  399.5 116.1 %copy-start.8 = (bf16[400,896]{1,0:T(8,128)(2,1)S(1)}, bf16[400,896]{1,0:T(8,128)(2,1)}, u32[]{:S(2)}) copy-start(bf16[400,896]{1,0:T(8,128)(2,1)} %param.12) | copy-start | bytes 2150404
  399.5 115.9 %all-to-all-start = ((bf16[2,400,896]{2,1,0:T(8,128)(2,1)}), bf16[2,400,896]{2,1,0:T(8,128)(2,1)S(1)}, u32[]{:S(2)}, u32[]{:S(2)}) async-start(bf16[2,400,896]{2,1,0:T(8,128)(2,1)} %bitcast.52), calls=%async_computation | async-start | bytes 2867200 | tf_op jit(solution)/shard_map/all_to_all | solution.py:29
  515.6 300.8 %copy-start.9 = (f32[28,4,896]{2,1,0:T(4,128)S(1)}, f32[28,4,896]{2,1,0:T(4,128)}, u32[]{:S(2)}) copy-start(f32[28,4,896]{2,1,0:T(4,128)} %param.13) | copy-start | bytes 1204228
  515.6 300.8 %copy-start.13 = (f32[28,4,896]{2,1,0:T(4,128)S(1)}, f32[28,4,896]{2,1,0:T(4,128)}, u32[]{:S(2)}) copy-start(f32[28,4,896]{2,1,0:T(4,128)} %param.14) | copy-start | bytes 1204228
  515.6 300.8 %copy-start.14 = (f32[28,4,896]{2,1,0:T(4,128)S(1)}, f32[28,4,896]{2,1,0:T(4,128)}, u32[]{:S(2)}) copy-start(f32[28,4,896]{2,1,0:T(4,128)} %param.15) | copy-start | bytes 1204228
  (6 other events, 19.7 us)
Sparse Core Ops, SparseCore 0:
  9.6 30.6 all-gather.7
  42.0 29.1 all-gather.3
  74.9 95.0 all-gather.5
  338.4 31.1 reduce-scatter.4
  371.8 32.8 reduce-scatter.6
  407.1 409.2 all-reduce.3
where the time goes:
time: 838 us; the launch traced here: 827 us
  waiting for transfers between devices  471 us (56%)
  local copies, waits for them, and re-layouts  119 us (14%)
  blocking collectives  110 us (13%)
  matrix products  78 us (9%)
  other arithmetic  29.4 us (4%)
  between operations  16.3 us (2%)
    unnamed x8, waiting for transfers between devices  298 us
    psum x1, blocking collectives, shards(): gain_sum, bias_sum = lax.psum((gain_part, bias_part), DP_MP)  110 us
    all_gather x1, waiting for transfers between devices, shards(): lax.all_gather(master.astype(jnp.bfloat16), DP, axis=0, tiled=True)  95.3 us
    all_gather x1, waiting for transfers between devices, shards(): lax.all_gather(cotangent, 'mp', axis=1, tiled=True)  28.1 us
    transpose x1, local copies, waits for them, and re-layouts, sum_by_chip(): parts = parts.reshape(*sizes, *inside).swapaxes(0, 1).reshape(-1, *inside)  27.8 us
    all_gather x1, waiting for transfers between devices, shards(): lax.all_gather(tokens, 'mp', axis=1, tiled=True)  26.4 us
    reduce_scatter x1, waiting for transfers between devices, sum_by_chip(): parts = lax.psum_scatter(parts, core, scatter_dimension=0, tiled=True)  22.6 us
    concatenate x1, local copies, waits for them, and re-layouts, shards(): jnp.concatenate([inner_piece, outer_piece[:, None]], axis=1)  21.7 us
  transfers between devices with their start and end apart: 7, of which 5 were waited for; matrix products, arithmetic and copies ran while one was open for 7% of the time, Pallas kernels for 0%

commit v1 on v0

v1 whole, which is shorter than its diff:
```python
import functools

import jax
import jax.numpy as jnp
from jax import lax
from jax.experimental import pallas as pl
from jax.experimental.pallas import tpu as pltpu
from jax.sharding import Mesh
from jax.sharding import PartitionSpec as P

HEADS = 8
HEAD_DIM = 112
PAD = 128
ROWS = 400
DIM = 1792
COLS = 896
BLOCK = 56
SHARD = 28
GROUPS = 64
DP = ("dp_0", "dp_1", "dp_2", "dp_3")
AXES = DP + ("mp",)
MESH = pl.DeviceIdType.MESH
N_SEMS = 224

eps_norm = 1e-06
beta_one = 0.9
beta_two = 0.95
learn_rate = 0.01
decay_rate = 0.1
adam_eps = 1e-08
step_count = 10.0

bf16 = jnp.bfloat16
f32 = jnp.float32

ORDER = (0, -1, 1, 2)
LEFT = pl.ds(0, 512)
RIGHT = pl.ds(512, 384)


def nt_dot(a, b):
    return lax.dot_general(a, b, (((1,), (1,)), ((), ())), preferred_element_type=f32)


def tn_dot(a, b):
    return lax.dot_general(a, b, (((0,), (0,)), ((), ())), preferred_element_type=f32)


def mod4(v):
    return lax.rem(v + 8, 4)


def block_kernel(
    tok, cot, wl, gain, bias, count, length,
    bo, ig, gout, ngout,
    W, xf, gf, xn, tn, tg, tnr, tgr, heads, outs, D, Dr,
    part, ra, sb, rb, rf, yb, yr, fs, fr, wsib, ops, opr, ips, ipr,
    mean_s, inv_s, nsrc, nr,
    ss, rs,
):
    z, yh, x, c, m = [lax.axis_index(a) for a in AXES]
    big, small = x + c * (z - x), z + c * (x - z)
    home, away = c == yh, c != yh

    def big_dev(d):
        return (mod4(z + c * d), yh, mod4(x + (1 - c) * d), c, m)

    def small_dev(d):
        return (mod4(z + (1 - c) * d), yh, mod4(x + c * d), c, m)

    sib = (z, yh, x, 1 - c, m)
    ypart = (z, 1 - yh, x, c, m)
    mate = (z, yh, x, c, 1 - m)

    index, pending = {}, []

    def message(name, src, dst, dev):
        k = index.setdefault(name, len(index))
        assert k < N_SEMS
        return pltpu.make_async_remote_copy(
            src_ref=src, dst_ref=dst, send_sem=ss.at[k], recv_sem=rs.at[k],
            device_id=dev, device_id_type=MESH,
        )

    def send(name, src, dst, dev):
        copy = message(name, src, dst, dev)
        copy.start()
        pending.append((copy.wait_send, None))

    def send_inside(when, name, build):
        message(name, *build()).start()
        pending.append((lambda: message(name, *build()).wait_send(), when))

    def recv(name, dst):
        message(name, dst, dst, sib).wait_recv()

    barrier = pltpu.get_barrier_semaphore()
    partners = (sib, ypart, mate, big_dev(1), big_dev(-1), small_dev(1), small_dev(-1))
    for dev in partners:
        pl.semaphore_signal(barrier, inc=1, device_id=dev, device_id_type=MESH)
    pl.semaphore_wait(barrier, len(partners))

    def cols(half):
        return pl.ds(pl.multiple_of(half * COLS, 128), COLS)

    def blk(i, j, cc=c):
        return i * (1 + 7 * cc) + j * (8 - 7 * cc) + 4 * cc

    own = blk(big, small)

    def spread(p, n, b):
        send(("b+", p, n), W.at[p, b], W.at[p, b], big_dev(1))
        send(("b-", p, n), W.at[p, b], W.at[p, b], big_dev(-1))
        send(("sib", p, n), W.at[p, b], W.at[p, b], sib)

    def gather_first(p):
        @pl.when(away)
        def _():
            send_inside(away, ("w", p), lambda: (wl.at[p], wsib.at[p], sib))

    def gather_own(p):
        @pl.when(home)
        def _():
            recv(("w", p), wsib.at[p])
            mine, other = wl[p].astype(f32), wsib[p].astype(f32)
            low = jnp.where(c == 0, mine, other)
            high = jnp.where(c == 0, other, mine)
            W[p, own] = jnp.concatenate([low, high], axis=0).astype(bf16)
            send_inside(home, ("y", p), lambda: (W.at[p, own], W.at[p, own], ypart))

        @pl.when(away)
        def _():
            recv(("y", p), W.at[p, own])

        send(("s+", p), W.at[p, own], W.at[p, own], small_dev(1))
        send(("s-", p), W.at[p, own], W.at[p, own], small_dev(-1))
        spread(p, 0, own)

    def gather_small(p):
        low, high, far = [blk(big, mod4(small + d)) for d in (-1, 1, 2)]
        recv(("s+", p), W.at[p, low])
        half = W.at[p, low, :, LEFT]
        send(("sf+", p), half, half, small_dev(1))
        spread(p, 1, low)
        recv(("s-", p), W.at[p, high])
        half = W.at[p, high, :, RIGHT]
        send(("sf-", p), half, half, small_dev(-1))
        spread(p, 2, high)
        recv(("sf+", p), W.at[p, far, :, LEFT])
        recv(("sf-", p), W.at[p, far, :, RIGHT])
        spread(p, 3, far)

    def gather_big(p):
        for n, d in enumerate(ORDER):
            j = mod4(small + d)
            b = blk(mod4(big - 1), j)
            recv(("b+", p, n), W.at[p, b])
            if n < 2:
                send(("f+", p, n), W.at[p, b], W.at[p, b], big_dev(1))
            send(("sib", p, 4 + n), W.at[p, b], W.at[p, b], sib)
            b = blk(mod4(big + 1), j)
            recv(("b-", p, n), W.at[p, b])
            if n >= 2:
                send(("f-", p, n), W.at[p, b], W.at[p, b], big_dev(-1))
            send(("sib", p, 8 + n), W.at[p, b], W.at[p, b], sib)

    def gather_far(p):
        for n, d in enumerate(ORDER):
            b = blk(mod4(big + 2), mod4(small + d))
            recv(("f+" if n < 2 else "f-", p, n), W.at[p, b])
            send(("sib", p, 12 + n), W.at[p, b], W.at[p, b], sib)

    def gather_done(p):
        for k, step in enumerate((0, -1, 1, 2)):
            for n, d in enumerate(ORDER):
                b = blk(mod4(small + step), mod4(big + d), 1 - c)
                recv(("sib", p, 4 * k + n), W.at[p, b])

    def weight(p):
        return W[p].reshape(DIM, COLS)

    def flip(src, dst):
        for h in range(2):
            dst[pl.ds(16 * h, 16)] = src[:, h * COLS : (h + 1) * COLS].T.reshape(16, BLOCK, ROWS)

    def to_sibling(name, src, dst):
        for k in range(4):
            send((name, k), src.at[pl.ds(8 * k + 4 * (1 - c), 4)], dst.at[pl.ds(4 * k, 4)], sib)

    def from_sibling(name, dst):
        for k in range(4):
            recv((name, k), dst.at[pl.ds(4 * k, 4)])

    live_count = (count[0] * length[0]).astype(f32)

    def live_rows(start, size):
        at = lax.broadcasted_iota(jnp.int32, (size, 1), 0).astype(f32) + float(start)
        return at < live_count

    def norm():
        def body(n, _):
            r = pl.ds(pl.multiple_of(n * 80, 16), 80)
            values = xf[r, :].astype(f32)
            center = jnp.mean(values, axis=-1, keepdims=True)
            shifted = values - center
            spread_ = jnp.mean(shifted * shifted, axis=-1, keepdims=True)
            inverse = lax.rsqrt(spread_ + eps_norm)
            mean_s[r, :] = center
            inv_s[r, :] = inverse
            xn[r, :] = (shifted * inverse * gain[...] + bias[...]).astype(bf16)
            return 0

        lax.fori_loop(0, ROWS // 80, body, 0)

    def split_heads(value, dst):
        low = value.astype(bf16)
        for h in range(HEADS):
            dst[h, :, :HEAD_DIM] = low[:, h * HEAD_DIM : (h + 1) * HEAD_DIM]
            dst[h, :, HEAD_DIM:] = jnp.zeros((ROWS, PAD - HEAD_DIM), bf16)

    def project(p, rows):
        split_heads(jnp.dot(rows[...], weight(p), preferred_element_type=f32), heads.at[p])

    scale = HEAD_DIM**-0.5

    def label(at):
        per = length[0].astype(f32)
        return jnp.where(at < live_count, jnp.floor((at + 0.5) / per), -1.0)

    def attention():
        down = lax.broadcasted_iota(jnp.int32, (ROWS, 1), 0).astype(f32)
        along = lax.broadcasted_iota(jnp.int32, (1, ROWS), 1).astype(f32)
        down, along = label(down), label(along)

        def body(h, _):
            qh, kh, vh, gh = heads[0, h], heads[1, h], heads[2, h], heads[3, h]
            s = jnp.where(down == along, nt_dot(qh, kh) * scale, -1e30)
            e = jnp.exp(s - jnp.max(s, axis=1, keepdims=True))
            prob = e * (1.0 / jnp.sum(e, axis=1, keepdims=True))
            low = prob.astype(bf16)
            outs[3, h] = jnp.dot(low, vh, preferred_element_type=f32).astype(bf16)
            dp = nt_dot(gh, vh)
            outs[2, h] = tn_dot(low, gh).astype(bf16)
            delta = jnp.sum(prob * dp, axis=1, keepdims=True)
            ds = (prob * (dp - delta) * scale).astype(bf16)
            outs[0, h] = jnp.dot(ds, kh, preferred_element_type=f32).astype(bf16)
            outs[1, h] = tn_dot(ds, qh).astype(bf16)
            return 0

        lax.fori_loop(0, HEADS, body, 0)

    def merge(p):
        for h in range(HEADS):
            D[p, :, h * HEAD_DIM : (h + 1) * HEAD_DIM] = outs[p, h][:, :HEAD_DIM]
        send(("D", p), D.at[p], Dr.at[p], sib)

    def half_weight(p, half):
        return W[p, pl.ds(16 * half, 16)].reshape(COLS, COLS)

    def out_projection():
        mixed = D[3]
        ops[...] = nt_dot(mixed, half_weight(3, 1 - m)).astype(bf16)
        send(("op",), ops, opr, mate)
        bo[...] = nt_dot(mixed, half_weight(3, m)).astype(bf16)

    def norm_backward():
        gain_sum = jnp.zeros((1, DIM), f32)
        bias_sum = jnp.zeros((1, DIM), f32)
        for start, size in ((0, 208), (208, 192)):
            r = pl.ds(start, size)
            ng = nt_dot(D[0, r, :], weight(0)) + nt_dot(D[1, r, :], weight(1))
            ng = ng + nt_dot(D[2, r, :], weight(2))
            normed = (xf[r, :].astype(f32) - mean_s[r, :]) * inv_s[r, :]
            gain_sum = gain_sum + jnp.sum(ng * normed, axis=0, keepdims=True)
            bias_sum = bias_sum + jnp.sum(ng, axis=0, keepdims=True)
            a = ng * gain[...]
            first = jnp.mean(a, axis=-1, keepdims=True)
            second = jnp.mean(a * normed, axis=-1, keepdims=True)
            ip = (inv_s[r, :] * (a - first - normed * second)).astype(bf16)
            ips[r, :] = jnp.where(m == 0, ip[:, COLS:], ip[:, :COLS])
            ig[r, :] = jnp.where(m == 0, ip[:, :COLS], ip[:, COLS:])
        send(("ip",), ips, ipr, mate)
        nsrc[0, 0:1, :] = gain_sum
        nsrc[0, 1:2, :] = bias_sum
        send(("n", 0), nsrc.at[0], nr.at[0, 0], sib)

    def norm_ring(k, pos, dev):
        send(("n+", k), nsrc.at[k], nr.at[k, pos], dev(1))
        send(("n-", k), nsrc.at[k], nr.at[k, pos], dev(-1))
        recv(("n+", k), nr.at[k, mod4(pos - 1)])
        send(("nf", k), nr.at[k, mod4(pos - 1)], nr.at[k, mod4(pos - 1)], dev(1))
        nr[k, pos] = nsrc[k]
        recv(("n-", k), nr.at[k, mod4(pos + 1)])
        recv(("nf", k), nr.at[k, mod4(pos + 2)])
        nsrc[k + 1] = (nr[k, 0] + nr[k, 1]) + (nr[k, 2] + nr[k, 3])

    def x_dev(d):
        return (z, yh, mod4(x + d), c, m)

    def z_dev(d):
        return (mod4(z + d), yh, x, c, m)

    def norm_sum_chip():
        recv(("n", 0), nr.at[0, 0])
        nsrc[1] = nsrc[0] + nr[0, 0]

    def norm_pair(k, dev):
        send(("n", k), nsrc.at[k], nr.at[k, 0], dev)
        recv(("n", k), nr.at[k, 0])
        nsrc[k + 1] = nsrc[k] + nr[k, 0]

    def grad_chunk(p, i):
        own_rows, sib_rows = (tg, tgr) if p == 3 else (tn, tnr)
        a = jnp.concatenate([own_rows[blk(i, j)] for j in range(4)], axis=0)
        b = jnp.concatenate([sib_rows[i * (1 + 3 * c) + j * (4 - 3 * c)] for j in range(4)], axis=0)
        v = jnp.dot(a, D[p], preferred_element_type=f32)
        v = v + jnp.dot(b, Dr[p], preferred_element_type=f32)
        part[p, i] = v.astype(bf16).reshape(4, BLOCK, COLS)

    lo, hi = pl.ds(0, 2), pl.ds(2, 2)
    nxt, prv, opp = mod4(big + 1), mod4(big - 1), mod4(big + 2)

    def grads(p):
        grad_chunk(p, opp)
        send(("1a", p), part.at[p, opp, lo], ra.at[p, 0], big_dev(1))
        send(("1b", p), part.at[p, opp, hi], ra.at[p, 1], big_dev(-1))
        grad_chunk(p, nxt)
        send(("2b", p), part.at[p, nxt, hi], ra.at[p, 2], big_dev(1))
        grad_chunk(p, prv)
        send(("2a", p), part.at[p, prv, lo], ra.at[p, 3], big_dev(-1))
        grad_chunk(p, big)

    def wide_add(p):
        recv(("1a", p), ra.at[p, 0])
        part[p, nxt, lo] = (part[p, nxt, lo].astype(f32) + ra[p, 0].astype(f32)).astype(bf16)
        send(("3a", p), part.at[p, nxt, lo], ra.at[p, 4], big_dev(1))
        recv(("1b", p), ra.at[p, 1])
        part[p, prv, hi] = (part[p, prv, hi].astype(f32) + ra[p, 1].astype(f32)).astype(bf16)
        send(("3b", p), part.at[p, prv, hi], ra.at[p, 5], big_dev(-1))

    def wide_sum(p):
        recv(("2b", p), ra.at[p, 2])
        recv(("2a", p), ra.at[p, 3])
        recv(("3a", p), ra.at[p, 4])
        recv(("3b", p), ra.at[p, 5])
        v = part[p, big, lo].astype(f32) + ra[p, 3].astype(f32) + ra[p, 4].astype(f32)
        sb[p, lo] = v.astype(bf16)
        v = part[p, big, hi].astype(f32) + ra[p, 2].astype(f32) + ra[p, 5].astype(f32)
        sb[p, hi] = v.astype(bf16)

    snx, spv, sop = mod4(small + 1), mod4(small - 1), mod4(small + 2)

    def narrow_send(q, p0, p1):
        send(("4a", q), sb.at[p0, sop], rb.at[q, 0], small_dev(1))
        send(("4b", q), sb.at[p1, sop], rb.at[q, 1], small_dev(-1))
        send(("5b", q), sb.at[p1, snx], rb.at[q, 2], small_dev(1))
        send(("5a", q), sb.at[p0, spv], rb.at[q, 3], small_dev(-1))

    def narrow_add(q, p0, p1):
        recv(("4a", q), rb.at[q, 0])
        sb[p0, snx] = (sb[p0, snx].astype(f32) + rb[q, 0].astype(f32)).astype(bf16)
        send(("6a", q), sb.at[p0, snx], rb.at[q, 4], small_dev(1))
        recv(("4b", q), rb.at[q, 1])
        sb[p1, spv] = (sb[p1, spv].astype(f32) + rb[q, 1].astype(f32)).astype(bf16)
        send(("6b", q), sb.at[p1, spv], rb.at[q, 5], small_dev(-1))

    def narrow_sum(q, p0, p1):
        recv(("5b", q), rb.at[q, 2])
        recv(("5a", q), rb.at[q, 3])
        recv(("6a", q), rb.at[q, 4])
        recv(("6b", q), rb.at[q, 5])
        rf[p0] = sb[p0, small].astype(f32) + rb[q, 3].astype(f32) + rb[q, 4].astype(f32)
        rf[p1] = sb[p1, small].astype(f32) + rb[q, 2].astype(f32) + rb[q, 5].astype(f32)
        for p in (p0, p1):
            over_y(p)

    def over_y(p):
        @pl.when(away)
        def _():
            yb[p] = rf[p].astype(bf16)
            send_inside(away, ("Y", p), lambda: (yb.at[p], yr.at[p], ypart))

    def finish(p):
        @pl.when(home)
        def _():
            recv(("Y", p), yr.at[p])
            v = rf[p] + yr[p].astype(f32)
            low, high = v[:SHARD], v[SHARD:]
            gout[p] = jnp.where(c == 0, low, high)
            fs[p] = jnp.where(c == 0, high, low)
            send_inside(home, ("F", p), lambda: (fs.at[p], fr.at[p], sib))

    def finish_other(p):
        @pl.when(away)
        def _():
            recv(("F", p), fr.at[p])
            gout[p] = fr[p]

    send(("tok",), tok, xf.at[:, cols(m)], mate)
    for p in range(4):
        gather_first(p)
    xf[:, cols(m)] = tok[...]
    gf[:, cols(m)] = cot[...]
    gather_own(0)
    gather_small(0)
    gather_own(1)
    gather_small(1)
    gather_big(0)
    gather_own(2)
    gather_far(0)
    recv(("tok",), xf.at[:, cols(1 - m)])
    send(("cot",), cot, gf.at[:, cols(m)], mate)
    gather_small(2)
    norm()
    gather_big(1)
    gather_own(3)
    flip(xn, tn)
    to_sibling("tn", tn, tnr)
    gather_far(1)
    gather_small(3)
    gather_done(0)
    project(0, xn)
    gather_big(2)
    gather_done(1)
    gather_far(2)
    project(1, xn)
    gather_big(3)
    gather_done(2)
    gather_far(3)
    project(2, xn)
    recv(("cot",), gf.at[:, cols(1 - m)])
    gf[...] = jnp.where(live_rows(0, ROWS), gf[...].astype(f32), 0.0).astype(bf16)
    flip(gf, tg)
    to_sibling("tg", tg, tgr)
    gather_done(3)
    project(3, gf)
    attention()
    for p in (3, 2, 0, 1):
        merge(p)
    from_sibling("tn", tnr)
    from_sibling("tg", tgr)
    recv(("D", 3), Dr.at[3])
    grads(3)
    out_projection()
    recv(("D", 2), Dr.at[2])
    grads(2)
    wide_add(3)
    recv(("D", 0), Dr.at[0])
    recv(("D", 1), Dr.at[1])
    norm_backward()
    wide_add(2)
    grads(0)
    wide_sum(3)
    wide_sum(2)
    narrow_send(0, 3, 2)
    grads(1)
    norm_sum_chip()
    wide_add(0)
    narrow_add(0, 3, 2)
    norm_ring(1, x, x_dev)
    wide_add(1)
    narrow_sum(0, 3, 2)
    norm_ring(2, z, z_dev)
    recv(("op",), opr)
    bo[...] = (tok[...].astype(f32) + (bo[...].astype(f32) + opr[...].astype(f32))).astype(bf16)
    norm_pair(3, mate)
    wide_sum(0)
    norm_pair(4, ypart)
    ngout[...] = nsrc[5]
    finish(3)
    finish(2)
    wide_sum(1)
    narrow_send(1, 0, 1)
    recv(("ip",), ipr)
    kept = jnp.where(live_rows(0, ROWS), cot[...].astype(f32), 0.0)
    ig[...] = (kept + (ig[...].astype(f32) + ipr[...].astype(f32))).astype(bf16)
    narrow_add(1, 0, 1)
    narrow_sum(1, 0, 1)
    finish(0)
    finish(1)
    for p in range(4):
        finish_other(p)

    for wait, when in pending:
        if when is None:
            wait()
        else:
            pl.when(when)(wait)


def run_block(tokens, cotangent, wl, gain, bias, image_count, tokens_per_image):
    vmem = pl.BlockSpec(memory_space=pltpu.VMEM)
    smem = pl.BlockSpec(memory_space=pltpu.SMEM)
    V = pltpu.VMEM
    return pl.pallas_call(
        block_kernel,
        out_shape=(
            jax.ShapeDtypeStruct((ROWS, COLS), bf16),
            jax.ShapeDtypeStruct((ROWS, COLS), bf16),
            jax.ShapeDtypeStruct((4, SHARD, COLS), f32),
            jax.ShapeDtypeStruct((2, DIM), f32),
        ),
        in_specs=[vmem] * 5 + [smem] * 2,
        out_specs=(vmem,) * 4,
        scratch_shapes=[
            V((4, 32, BLOCK, COLS), bf16),
            V((ROWS, DIM), bf16),
            V((ROWS, DIM), bf16),
            V((ROWS, DIM), bf16),
            V((32, BLOCK, ROWS), bf16),
            V((32, BLOCK, ROWS), bf16),
            V((16, BLOCK, ROWS), bf16),
            V((16, BLOCK, ROWS), bf16),
            V((4, HEADS, ROWS, PAD), bf16),
            V((4, HEADS, ROWS, PAD), bf16),
            V((4, ROWS, COLS), bf16),
            V((4, ROWS, COLS), bf16),
            V((4, 4, 4, BLOCK, COLS), bf16),
            V((4, 6, 2, BLOCK, COLS), bf16),
            V((4, 4, BLOCK, COLS), bf16),
            V((2, 6, BLOCK, COLS), bf16),
            V((4, BLOCK, COLS), f32),
            V((4, BLOCK, COLS), bf16),
            V((4, BLOCK, COLS), bf16),
            V((4, SHARD, COLS), f32),
            V((4, SHARD, COLS), f32),
            V((4, SHARD, COLS), bf16),
            V((ROWS, COLS), bf16),
            V((ROWS, COLS), bf16),
            V((ROWS, COLS), bf16),
            V((ROWS, COLS), bf16),
            V((ROWS, 1), f32),
            V((ROWS, 1), f32),
            V((6, 2, DIM), f32),
            V((5, 4, 2, DIM), f32),
            pltpu.SemaphoreType.DMA((N_SEMS,)),
            pltpu.SemaphoreType.DMA((N_SEMS,)),
        ],
        compiler_params=pltpu.CompilerParams(
            collective_id=0, has_side_effects=True, vmem_limit_bytes=67043328
        ),
        name="block",
    )(tokens, cotangent, wl, gain, bias, image_count, tokens_per_image)


def adam_update(weight_now, moment_first, moment_second, gradient, decay):
    first_new = beta_one * moment_first + (1.0 - beta_one) * gradient
    second_new = beta_two * moment_second + (1.0 - beta_two) * gradient * gradient
    first_hat = first_new / (1.0 - beta_one**step_count)
    second_hat = second_new / (1.0 - beta_two**step_count)
    weight_new = weight_now - learn_rate * (
        first_hat / (jnp.sqrt(second_hat) + adam_eps) + decay * weight_now
    )
    return (weight_new, first_new, second_new)


def shards(
    tokens,
    cotangent,
    master,
    moment_one,
    moment_two,
    ln_gain,
    ln_bias,
    norm_moment_one,
    norm_moment_two,
    image_count,
    tokens_per_image,
):
    wl = jnp.transpose(master.astype(bf16), (1, 0, 2))
    block_out, input_grad, grad, norm_sums = run_block(
        tokens, cotangent, wl, ln_gain[None], ln_bias[None], image_count, tokens_per_image
    )
    weight_grad = jnp.transpose(grad, (1, 0, 2)) / GROUPS
    new_master, new_moment_one, new_moment_two = adam_update(
        master, moment_one, moment_two, weight_grad, decay_rate
    )
    stacked_params = jnp.stack([ln_gain, ln_bias])
    new_norm, new_norm_moment_one, new_norm_moment_two = adam_update(
        stacked_params, norm_moment_one, norm_moment_two, norm_sums / GROUPS, 0.0
    )
    return (
        block_out,
        input_grad,
        new_master,
        new_moment_one,
        new_moment_two,
        new_norm[0],
        new_norm[1],
        new_norm_moment_one,
        new_norm_moment_two,
    )


def solution(mesh):
    finer = Mesh(mesh.devices.reshape(4, 2, 4, 2, mesh.shape["mp"]), AXES)
    return jax.shard_map(
        shards,
        mesh=finer,
        in_specs=(
            P(DP, "mp"),
            P(DP, "mp"),
            P(DP, None, "mp"),
            P(DP, None, "mp"),
            P(DP, None, "mp"),
            P(),
            P(),
            P(),
            P(),
            P(DP),
            P(DP),
        ),
        out_specs=(
            P(DP, "mp"),
            P(DP, "mp"),
            P(DP, None, "mp"),
            P(DP, None, "mp"),
            P(DP, None, "mp"),
            P(),
            P(),
            P(),
            P(),
        ),
        check_vma=False,
    )
```

time: 838 us -> 176 us (0.21); the launches traced: 827 us -> 174 us
  waiting for transfers between devices: 471 us -> 0 us
  Pallas kernels: 0 us -> 161 us
  local copies, waits for them, and re-layouts: 119 us -> 7.93 us
  blocking collectives: 110 us -> 0 us
  matrix products: 78 us -> 0 us
  other arithmetic: 29.4 us -> 3.48 us
  between operations: 16.3 us -> 2 us
    unnamed x8 -> x0, waiting for transfers between devices: 298 us -> none
    pallas_call x0 -> x1, Pallas kernels: none -> 161 us  [run_block(): pl.pallas_call(block_kernel, out_shape=(jax.ShapeDtypeStruct((ROWS, COLS)...]
    all_gather x3 -> x0, waiting for transfers between devices: 150 us -> none  [the longest x1 95.3 us: shards(): lax.all_gather(master.astype(jnp.bfloat16), DP, axis=0, tiled=True)]
    psum x1 -> x0, blocking collectives: 110 us -> none  [shards(): gain_sum, bias_sum = lax.psum((gain_part, bias_part), DP_MP)]
    dot_general x12 -> x0, matrix products: 78 us -> none  [the longest x1 12.7 us: shards(): jnp.einsum('hqk,khd->qhd', score_grad, key_rows, preferred_element_type=j...]
    transpose x1 -> x0, local copies, waits for them, and re-layouts: 27.8 us -> none  [sum_by_chip(): parts = parts.reshape(*sizes, *inside).swapaxes(0, 1).reshape(-1, *inside)]
    reduce_scatter x1 -> x0, waiting for transfers between devices: 22.6 us -> none  [sum_by_chip(): parts = lax.psum_scatter(parts, core, scatter_dimension=0, tiled=True)]
    concatenate x1 -> x0, local copies, waits for them, and re-layouts: 21.7 us -> none  [shards(): jnp.concatenate([inner_piece, outer_piece[:, None]], axis=1)]
  transfers between devices with their start and end apart: 7 -> 0, of which waited for: 5 -> 0; matrix products, arithmetic and copies ran while one was open for 7% -> 0% of each run, Pallas kernels for 0% -> 0%
where the time goes in v1:
time: 176 us; the launch traced here: 174 us
  Pallas kernels  161 us (91%)
  local copies, waits for them, and re-layouts  7.93 us (5%)
  other arithmetic  3.48 us (2%)
  between operations  2 us (1%)
    pallas_call x1, Pallas kernels, run_block(): pl.pallas_call(block_kernel, out_shape=(jax.ShapeDtypeStruct((ROWS, COLS)...  161 us
    unnamed x23, local copies, waits for them, and re-layouts  5.38 us

profile of v1, /device:TPU:0, one launch (start us, length us, event | category | flops | bytes accessed | tf_op | source)
XLA Modules:
  0.0 174.4 jit_solution(383302960283400724)
XLA Ops:
  0.6 1.1 convert_element_type.3
  1.7 0.0 copy-start.7
  1.7 0.7 copy.53
  2.4 0.0 copy-done.7
  2.4 0.6 broadcast_in_dim.6.gain
  3.0 0.1 copy-done.8
  3.1 0.6 broadcast_in_dim.7.bias
  5.0 161.0 %block.1 = (bf16[400,896]{1,0:T(8,128)(2,1)}, bf16[400,896]{1,0:T(8,128)(2,1)}, f32[4,28,896]{2,1,0:T(8,128)}, f32[2,1792]{1,0:T(2,128)}) custom-call(bf16[400,896]{1,0:T(8,128)(2,1)} %tok.1, bf16[400,896]{1,0:T(8,128)(2,1)} %cot.1, bf16[4,28,896]{2,1,0:T(8,128)(2,1)} %bitcast.9, f32[1,1792]{1,0:T(1,128)} %broadcast_in_dim.6.gain, ...), custom_call_target="tpu_custom_call" | custom-call | tf_op jit(solution)/shard_map/block/pallas_call | solution.py:495
  166.0 1.8 %copy_subtract_fusion = (f32[28,4,896]{2,0,1:T(8,128)S(1)}, f32[28,4,896]{2,0,1:T(8,128)S(1)}, f32[28,4,896]{2,0,1:T(8,128)S(1)}) fusion(f32[28,4,896]{2,1,0:T(4,128)} %param.13, f32[4,28,896]{2,1,0:T(8,128)} %get-tuple-element.15, f32[28,4,896]{2,1,0:T(4,128)} %param.14, f32[28,4,896]{2,1,0:T(4,128)} %param.15), kind=kLoop, calls=%fused_computation.1 | loop fusion | flops 1605632 | bytes 2809856 | tf_op jit(solution)/shard_map/sub | solution.py:551
  167.8 1.0 copy.33
  168.8 1.0 copy.34
  169.8 0.0 copy-start.5
  169.8 0.0 copy-start.6
  169.9 1.0 copy.35
  170.9 0.0 copy-done.2
  170.9 0.0 copy-done.3
  170.9 0.0 copy-done.4
  170.9 0.0 copy-done.5
  170.9 0.0 copy-done.6
  170.9 0.7 multiply_subtract_fusion
  171.5 0.6 slice_reduce_fusion
  172.2 0.9 copy.58
  173.0 0.5 copy-done
  173.6 0.9 copy.59
  (7 shorter events, 0.0 us)
Async XLA Ops:
  1.7 0.7 copy-start.7
  2.4 0.7 copy-start.8
  169.8 2.4 %copy-start.1 = (bf16[400,896]{1,0:T(8,128)(2,1)S(1)}, bf16[400,896]{1,0:T(8,128)(2,1)}, u32[]{:S(2)}) copy-start(bf16[400,896]{1,0:T(8,128)(2,1)} %get-tuple-element.52) | copy-start | bytes 2150404
  169.8 1.0 copy-start.2
  169.8 1.0 copy-start.3
  169.8 1.0 copy-start.4
  169.8 1.0 copy-start.5
  169.8 1.0 copy-start.6
  172.2 1.4 copy-start
